TPU v7x, 256 devices: a whole 4x4x8 slice. The times are simulated.
256 devices in a mesh: box: 64 (over x, z, core), blk: 4 (over y).
Axes of the slice: x: 4, y: 4, z: 8, core: 2. Of those that a mesh axis runs over, the one named last changes fastest.
Arguments:
- operator_map: float32 [64, 1536, 1536], P('box', 'blk'), may hold values from -0.5 to 2, as said below
- face_list: int32 [64, 256], replicated, may hold values from 0 to 1535, as said below
Outputs:
- merged: float32 [64, 1536, 3072], P('box', 'blk')
Inputs may be any that keep to these rules, and one draw needn't show every extreme that they name: `operator_map`: each box's map is symmetric; its diagonal lies in 1 to 2. Points 6 i + f and 6 j + f with the same f lie on one face: their entry is zero unless |i - j| is 1 or 2, and then lies in -0.245 to -0.12. Entries between points of different faces lie in -0.5 to 0.5. `face_list`: entry i of box b's list is 6 i + f_b with f_b from 0 to 5, so each list rises; boxes 2p and 2p + 1 list opposite faces, f = 2 a + 1 and f = 2 a, with one a from 0 to 2 for each pair, entry i of one facing entry i of the other.
All inputs are finite; a program needn't handle non-finite values.
Results may differ from a plain program's by a relative error of at most 0.0003.
Values sent between devices are 32-bit elements; how exact they have to be, the bound alone decides.
A program may use at most 64 MiB of HBM per device.

v0:
```python
import jax
import jax.numpy as jnp
from jax import lax
from jax.sharding import PartitionSpec as P


def from_partner(block, axis, apart):
    count = lax.axis_size(axis)
    route = []
    for low in range(count):
        high = low | 1 << apart
        if high != low and high < count:
            route += [(low, high), (high, low)]
    return lax.ppermute(block, axis, route)


def on_device(operator_map, face_list):
    blocks = lax.axis_size("blk")
    box_index = lax.axis_index("box")
    blk_index = lax.axis_index("blk")
    local_rows = operator_map[0]
    row_count = local_rows.shape[0]
    face_size = face_list.shape[1]
    per_block = face_size // blocks
    own_list = lax.dynamic_index_in_dim(face_list, box_index, 0, keepdims=False)
    sibling_index = jnp.bitwise_xor(box_index, 1)
    sibling_list = lax.dynamic_index_in_dim(face_list, sibling_index, 0, keepdims=False)
    local_list = (
        lax.dynamic_slice_in_dim(own_list, blk_index * per_block, per_block) - blk_index * row_count
    )
    picked = jnp.take(local_rows, local_list, axis=0)
    face_block = lax.all_gather(picked, "blk", axis=0, tiled=True)
    own_face = jnp.take(face_block, own_list, axis=1)
    is_lower = jnp.bitwise_and(box_index, 1) == 0
    coupling = jnp.take(local_rows, own_list, axis=1)
    sibling_block = from_partner(face_block, "box", 0)
    schur_sum = own_face + jnp.take(sibling_block, sibling_list, axis=1)
    factor = jnp.linalg.cholesky(schur_sum)
    lower_part = jnp.where(is_lower, face_block, sibling_block)
    upper_part = jnp.where(is_lower, sibling_block, face_block)
    weights = jax.scipy.linalg.cho_solve((factor, True), coupling.T).T
    correction = jnp.dot(
        weights,
        jnp.concatenate([lower_part, upper_part], axis=1),
        precision=lax.Precision.HIGHEST,
        preferred_element_type=jnp.float32,
    )
    blank_rows = jnp.zeros_like(local_rows)
    diagonal_part = jnp.concatenate(
        [jnp.where(is_lower, local_rows, blank_rows), jnp.where(is_lower, blank_rows, local_rows)],
        axis=1,
    )
    return (diagonal_part - correction)[None, :, :]


def solution(mesh):
    in_specs = (P("box", "blk", None), P())
    out_specs = P("box", "blk", None)
    return jax.shard_map(
        on_device, mesh=mesh, in_specs=in_specs, out_specs=out_specs, check_vma=False
    )
```

profile of v0, /device:TPU:1, one launch (start us, length us, event | category | flops | bytes accessed | tf_op | source)
XLA Modules:
  0.0 132.3 jit_solution(14960521785130965118)
XLA Ops:
  6.5 0.0 all-gather.2.cloned.1.call-start
  6.5 0.8 compare_and_fusion.2
  7.3 0.0 copy-start
  7.3 2.7 %gather_fusion = f32[64,1536]{1,0:T(8,128)S(1)} fusion(f32[384,1536]{1,0:T(8,128)} %bitcast.56, s32[1024]{0:T(1024)S(1)} %pad_clamp_fusion.3), kind=kCustom, calls=%fused_computation.2 | custom fusion | bytes 786688 | tf_op jit(solution)/shard_map/jit(_take)/gather | solution.py:31
  10.1 0.9 broadcast_select_fusion.5
  10.9 0.0 all-gather.2.cloned.1.call-update
  11.0 0.0 copy-done
  11.0 2.0 %copy.10 = f32[384,1536]{0,1:T(8,128)} copy(f32[384,1536]{1,0:T(8,128)S(1)} %bitcast.57) | data formatting | bytes 4718592 | tf_op jit(solution)/shard_map/squeeze | solution.py:21
  12.9 0.7 compare_select_fusion
  13.6 2.8 %gather_fusion.1 = f32[256,384]{1,0:T(8,128)S(1)} fusion(f32[384,1536]{0,1:T(8,128)} %copy.10, s32[1024]{0:T(1024)S(1)} %pad_clamp_fusion), kind=kCustom, calls=%fused_computation.3 | custom fusion | bytes 787456 | tf_op jit(solution)/shard_map/jit(_take)/gather | solution.py:35
  16.4 0.7 constant_dynamic-slice_fusion.1
  17.2 26.8 %all-gather.2.cloned.1.call-done = f32[256,1536]{1,0:T(8,128)} async-done(((f32[64,1536]{1,0:T(8,128)}), f32[256,1536]{1,0:T(8,128)}) %all-gather.2.cloned.1.call-update) | async-done | bytes 1572880 | tf_op jit(solution)/shard_map/all_gather | solution.py:32
  44.0 0.7 collective-permute-start
  44.7 0.1 broadcast_select_fusion.4
  44.8 2.9 %broadcast_select_fusion.1 = (f32[384,1536]{1,0:T(8,128)}, f32[384,1536]{1,0:T(8,128)}) fusion(pred[]{:T(512)S(6)} %eq.3, f32[1,384,1536]{2,1,0:T(8,128)S(1)} %copy-done), kind=kLoop, calls=%fused_computation.12 | loop fusion | flops 1179648 | bytes 7077889 | tf_op jit(solution)/shard_map/jit(_where)/select_n | solution.py:50
  47.7 1.9 %copy.7 = f32[256,1536]{0,1:T(8,128)S(1)} copy(f32[256,1536]{1,0:T(8,128)} %all-gather.2.cloned.1.call-done) | data formatting | bytes 3145728 | tf_op jit(solution)/shard_map/all_gather | solution.py:32
  49.6 1.0 gather_fusion.2
  50.5 0.0 collective-permute-done
  50.5 1.9 %copy.8 = f32[256,1536]{0,1:T(8,128)S(1)} copy(f32[256,1536]{1,0:T(8,128)} %collective-permute-done) | data formatting | bytes 3145728 | tf_op jit(solution)/shard_map/ppermute | solution.py:14
  52.4 1.0 gather_fusion.3
  53.4 0.1 bitcast_add_fusion.1
  53.5 0.1 copy.9
  53.7 11.7 %cholesky.50 = f32[128,128]{1,0:T(8,128)S(1)} custom-call(f32[128,128]{1,0:T(8,128)S(1)} %cholesky.118), custom_call_target="Cholesky" | custom-call | tf_op jit(solution)/shard_map/jit(cholesky)/cholesky | solution.py:38
  65.5 0.7 compare_reduce_fusion.1
  66.2 9.8 %custom-call.18 = f32[1,128,128]{1,2,0:T(8,128)S(1)} custom-call(f32[1,128,128]{2,1,0:T(8,128)S(1)} %get-tuple-element.35), custom_call_target="InvertDiagBlocksLowerTriangular" | custom-call | tf_op jit(solution)/shard_map/jit(cholesky)/cholesky | solution.py:38
  76.0 0.2 constant_dynamic-update-slice_fusion
  76.2 0.3 convolution_subtract_fusion.2
  76.5 0.0 copy-start.3
  76.5 11.9 %cholesky.105 = f32[128,128]{1,0:T(8,128)S(1)} custom-call(f32[128,128]{1,0:T(8,128)S(1)} %convolution_subtract_fusion.2), custom_call_target="Cholesky" | custom-call | tf_op jit(solution)/shard_map/jit(cholesky)/cholesky | solution.py:38
  88.4 0.6 compare_reduce_fusion
  90.3 0.1 triangular_solve.70
  90.4 4.1 %while.1 = (s32[]{:T(128)}, f32[256,256]{1,0:T(8,128)S(1)}, s32[2,2]{1,0:T(2,128)S(1)}, f32[2,128,128]{2,1,0:T(8,128)S(1)}, s32[]{:T(128)}) while((s32[]{:T(128)}, f32[256,256]{1,0:T(8,128)S(1)}, s32[2,2]{1,0:T(2,128)S(1)}, f32[2,128,128]{2,1,0:T(8,128)S(1)}, s32[]{:T(128)}) %tuple.28), condition=%wide.while_cond, body=%wide.while_body.sunk | while | flops 2 | bytes 131189 | solution.py:41
  90.4 0.7 fusion.29
  91.1 1.3 %bitcast_dynamic-update-slice_fusion.2 = f32[2,128,128]{2,1,0:T(8,128)S(1)} fusion(f32[2,128,128]{2,1,0:T(8,128)S(1)} %get-tuple-element.77, s32[]{:T(128)S(6)} %copy.16, f32[256,256]{1,0:T(8,128)S(1)} %get-tuple-element.80, s32[]{:T(128)} %bitcast.54, s32[]{:T(128)} %bitcast.55), kind=kLoop, calls=%fused_computation.4.clone.1 | loop fusion | bytes 131084 | tf_op jit(solution)/shard_map/jit(_cho_solve)/triangular_solve
  92.5 0.7 fusion.29
  93.1 1.3 %bitcast_dynamic-update-slice_fusion.2 = f32[2,128,128]{2,1,0:T(8,128)S(1)} fusion(f32[2,128,128]{2,1,0:T(8,128)S(1)} %get-tuple-element.77, s32[]{:T(128)S(6)} %copy.16, f32[256,256]{1,0:T(8,128)S(1)} %get-tuple-element.80, s32[]{:T(128)} %bitcast.54, s32[]{:T(128)} %bitcast.55), kind=kLoop, calls=%fused_computation.4.clone.1 | loop fusion | bytes 131084 | tf_op jit(solution)/shard_map/jit(_cho_solve)/triangular_solve
  94.5 19.7 %custom-call.19 = f32[2,128,128]{1,2,0:T(8,128)S(1)} custom-call(f32[2,128,128]{2,1,0:T(8,128)S(1)} %get-tuple-element.13), custom_call_target="InvertDiagBlocksLowerTriangular" | custom-call | tf_op jit(solution)/shard_map/jit(_cho_solve)/triangular_solve | solution.py:41
  114.2 0.4 fusion.8
  114.5 0.3 convolution_subtract_fusion.1
  114.9 0.4 fusion.15
  115.2 0.3 fusion.14
  115.6 0.4 convolution_subtract_fusion
  115.9 0.3 fusion.13
  116.3 0.0 copy-done.3
  116.3 0.0 copy-start.1
  116.3 0.0 copy-start.2
  116.3 1.8 %broadcast_select_fusion.3 = (f32[256,1536]{1,0:T(8,128)S(1)}, f32[256,1536]{1,0:T(8,128)S(1)}) fusion(f32[256,1536]{1,0:T(8,128)S(1)} %copy-done.3, f32[256,1536]{1,0:T(8,128)} %collective-permute-done, pred[]{:T(512)S(6)} %eq.3), kind=kLoop, calls=%fused_computation.17 | loop fusion | flops 786432 | bytes 6291457 | tf_op jit(solution)/shard_map/jit(_where)/select_n | solution.py:39
  118.1 0.3 copy-done.1
  118.4 0.7 copy-done.2
  119.1 6.4 %fusion = f32[1,384,3072]{2,1,0:T(8,128)} fusion(f32[384,1536]{1,0:T(8,128)S(1)} %copy-done.2, f32[384,1536]{1,0:T(8,128)S(1)} %copy-done.1, f32[256,1536]{1,0:T(8,128)S(1)} %get-tuple-element.29, f32[256,1536]{1,0:T(8,128)S(1)} %get-tuple-element.28, f32[128,384]{1,0:T(8,128)S(1)} %fusion.14, f32[128,384]{1,0:T(8,128)S(1)} %fusion.13), kind=kOutput, calls=%fused_computation.7 | convolution fusion | flops 3627122688 | bytes 12976128 | tf_op jit(solution)/shard_map/dot_general | solution.py:42
  (18 shorter events, 0.2 us)
Async XLA Ops:
  6.5 37.5 %all-gather.2.cloned.1.call-start = ((), (), s32[]{:S(2)}) async-start(), calls=%async_computation | async-start | bytes 1966080 | tf_op jit(solution)/shard_map/all_gather | solution.py:32
  7.3 3.6 %copy-start = (f32[1,384,1536]{2,1,0:T(8,128)S(1)}, f32[1,384,1536]{2,1,0:T(8,128)}, u32[]{:S(2)}) copy-start(f32[1,384,1536]{2,1,0:T(8,128)} %param.4) | copy-start | bytes 7077892
  44.0 6.5 %collective-permute-start = (f32[256,1536]{1,0:T(8,128)}, f32[256,1536]{1,0:T(8,128)}, u32[]{:S(2)}, u32[]{:S(2)}) collective-permute-start(f32[256,1536]{1,0:T(8,128)} %all-gather.2.cloned.1.call-done), channel_id=1, source_target_pairs={{0,4},{4,0},{8,12},{12,8},{16,20},{20,16},{24,28},{28,24},{32,36},... | collective-permute-start | bytes 4718600 | tf_op jit(solution)/shard_map/ppermute | solution.py:14
  76.5 39.7 %copy-start.3 = (f32[256,1536]{1,0:T(8,128)S(1)}, f32[256,1536]{1,0:T(8,128)}, u32[]{:S(2)}) copy-start(f32[256,1536]{1,0:T(8,128)} %all-gather.2.cloned.1.call-done) | copy-start | bytes 4718596
  116.3 2.1 %copy-start.1 = (f32[384,1536]{1,0:T(8,128)S(1)}, f32[384,1536]{1,0:T(8,128)}, u32[]{:S(2)}) copy-start(f32[384,1536]{1,0:T(8,128)} %get-tuple-element.30) | copy-start | bytes 7077892
  116.3 2.8 %copy-start.2 = (f32[384,1536]{1,0:T(8,128)S(1)}, f32[384,1536]{1,0:T(8,128)}, u32[]{:S(2)}) copy-start(f32[384,1536]{1,0:T(8,128)} %get-tuple-element.31) | copy-start | bytes 7077892
Sparse Core Ops, SparseCore 0:
  11.1 32.8 all-gather.1
where the time goes:
time: 133 us; the launch traced here: 132 us
  other arithmetic  61.8 us (46%)
  waiting for transfers between devices  26.9 us (20%)
  local copies, waits for them, and re-layouts  19.1 us (14%)
  between operations  14.9 us (11%)
  matrix products  8.89 us (7%)
    another operation x7, other arithmetic, on_device(): factor = jnp.linalg.cholesky(schur_sum)  34.8 us
    all_gather x1, waiting for transfers between devices, on_device(): face_block = lax.all_gather(picked, 'blk', axis=0, tiled=True)  26.8 us
    another operation x3, other arithmetic, on_device(): weights = jax.scipy.linalg.cho_solve((factor, True), coupling.T).T  19.7 us
    dot_general x1, matrix products, on_device(): jnp.dot(weights, jnp.concatenate([lower_part, upper_part], axis=1), preci...  6.37 us
    another operation x6, local copies, waits for them, and re-layouts  4.03 us
    select_n x1, other arithmetic, on_device(): jnp.where(is_lower, local_rows, blank_rows)  2.87 us
    gather x1, local copies, waits for them, and re-layouts, on_device(): coupling = jnp.take(local_rows, own_list, axis=1)  2.8 us
    gather x1, local copies, waits for them, and re-layouts, on_device(): picked = jnp.take(local_rows, local_list, axis=0)  2.71 us
  transfers between devices with their start and end apart: 2, of which 1 were waited for; matrix products, arithmetic and copies ran while one was open for 9% of the time, Pallas kernels for 0%

commit v1 on v0

--- a/solution.py
+++ b/solution.py
@@ -2,6 +2,11 @@
 import jax.numpy as jnp
 from jax import lax
 from jax.sharding import PartitionSpec as P
+
+
+def swapped_in(x, name, d):
+    outgoing = jnp.stack([x] * lax.axis_size(name))
+    return jnp.concatenate(lax.all_to_all(outgoing, name, 0, 0), axis=d)
 
 
 def from_partner(block, axis, apart):
@@ -29,7 +34,7 @@
         lax.dynamic_slice_in_dim(own_list, blk_index * per_block, per_block) - blk_index * row_count
     )
     picked = jnp.take(local_rows, local_list, axis=0)
-    face_block = lax.all_gather(picked, "blk", axis=0, tiled=True)
+    face_block = swapped_in(picked, "blk", 0)
     own_face = jnp.take(face_block, own_list, axis=1)
     is_lower = jnp.bitwise_and(box_index, 1) == 0
     coupling = jnp.take(local_rows, own_list, axis=1)

time: 133 us -> 119 us (0.89)
  waiting for transfers between devices: 26.9 us -> 12.3 us
  between operations: 14.9 us -> 1.54 us
  starting transfers between devices: 0.68 us -> 8.39 us
  matrix products: 8.89 us -> 12.4 us
  local copies, waits for them, and re-layouts: 19.1 us -> 22.4 us
    all_gather x1 -> x0, waiting for transfers between devices: 26.8 us -> none  [on_device(): face_block = lax.all_gather(picked, 'blk', axis=0, tiled=True)]
    all_to_all x0 -> x1, waiting for transfers between devices: none -> 12.3 us  [swapped_in(): return jnp.concatenate(lax.all_to_all(outgoing, name, 0, 0), axis=d)]
    all_to_all x0 -> x1, starting transfers between devices: none -> 5 us  [swapped_in(): return jnp.concatenate(lax.all_to_all(outgoing, name, 0, 0), axis=d)]
    dot_general x1, matrix products: 6.37 us -> 9.86 us  [on_device(): jnp.dot(weights, jnp.concatenate([lower_part, upper_part], axis=1), preci...]
    reshape x0 -> x1, local copies, waits for them, and re-layouts: none -> 3.01 us  [swapped_in(): return jnp.concatenate(lax.all_to_all(outgoing, name, 0, 0), axis=d)]
    ppermute x1, starting transfers between devices: 0.68 us -> 3.38 us  [from_partner(): return lax.ppermute(block, axis, route)]
    ppermute x1 -> x0, local copies, waits for them, and re-layouts: 1.87 us -> none  [from_partner(): return lax.ppermute(block, axis, route)]
    all_gather x1 -> x0, local copies, waits for them, and re-layouts: 1.87 us -> none  [on_device(): face_block = lax.all_gather(picked, 'blk', axis=0, tiled=True)]
  transfers between devices with their start and end apart: 2 -> 2, of which waited for: 1 -> 1; matrix products, arithmetic and copies ran while one was open for 9% -> 10% of each run, Pallas kernels for 0% -> 0%
where the time goes in v1:
time: 119 us; the launch traced here: 118 us
  other arithmetic  60.9 us (51%)
  local copies, waits for them, and re-layouts  22.4 us (19%)
  matrix products  12.4 us (10%)
  waiting for transfers between devices  12.3 us (10%)
  starting transfers between devices  8.39 us (7%)
  between operations  1.54 us (1%)
    another operation x7, other arithmetic, on_device(): factor = jnp.linalg.cholesky(schur_sum)  34.7 us
    another operation x3, other arithmetic, on_device(): weights = jax.scipy.linalg.cho_solve((factor, True), coupling.T).T  19.7 us
    all_to_all x1, waiting for transfers between devices, swapped_in(): return jnp.concatenate(lax.all_to_all(outgoing, name, 0, 0), axis=d)  12.3 us
    dot_general x1, matrix products, on_device(): jnp.dot(weights, jnp.concatenate([lower_part, upper_part], axis=1), preci...  9.86 us
    all_to_all x1, starting transfers between devices, swapped_in(): return jnp.concatenate(lax.all_to_all(outgoing, name, 0, 0), axis=d)  5 us
    another operation x6, local copies, waits for them, and re-layouts  3.99 us
    ppermute x1, starting transfers between devices, from_partner(): return lax.ppermute(block, axis, route)  3.38 us
    reshape x1, local copies, waits for them, and re-layouts, swapped_in(): return jnp.concatenate(lax.all_to_all(outgoing, name, 0, 0), axis=d)  3.01 us
  transfers between devices with their start and end apart: 2, of which 1 were waited for; matrix products, arithmetic and copies ran while one was open for 10% of the time, Pallas kernels for 0%

profile of v1, /device:TPU:1, one launch (start us, length us, event | category | flops | bytes accessed | tf_op | source)
XLA Modules:
  0.0 118.1 jit_solution(4244030206186329736)
XLA Ops:
  0.0 0.8 compare_and_fusion.2
  0.8 2.6 %gather_fusion = f32[64,1536]{1,0:T(8,128)S(1)} fusion(f32[384,1536]{1,0:T(8,128)} %bitcast.57, s32[1024]{0:T(1024)S(1)} %pad_clamp_fusion.3), kind=kCustom, calls=%fused_computation.2 | custom fusion | bytes 786688 | tf_op jit(solution)/shard_map/jit(_take)/gather | solution.py:36
  3.4 0.1 broadcast_select_fusion.5
  3.5 0.0 copy-start
  3.5 1.3 %stack.2 = f32[4,64,1536]{2,1,0:T(8,128)} broadcast(f32[64,1536]{1,0:T(8,128)S(1)} %broadcast_select_fusion.5), dimensions={1,2} | broadcast | bytes 1966080 | tf_op jit(solution)/shard_map/stack | solution.py:8
  4.8 5.0 %all-to-all-start = ((f32[4,64,1536]{2,1,0:T(8,128)}), f32[4,64,1536]{2,1,0:T(8,128)}, u32[]{:S(2)}, u32[]{:S(2)}) async-start(f32[4,64,1536]{2,1,0:T(8,128)} %stack.2), calls=%async_computation | async-start | bytes 3145728 | tf_op jit(solution)/shard_map/all_to_all | solution.py:9
  9.8 0.0 copy-done
  9.8 1.9 %copy.9 = f32[384,1536]{0,1:T(8,128)} copy(f32[384,1536]{1,0:T(8,128)S(1)} %bitcast.58) | data formatting | bytes 4718592 | tf_op jit(solution)/shard_map/squeeze | solution.py:26
  11.8 0.7 compare_select_fusion
  12.5 2.8 %gather_fusion.1 = f32[256,384]{1,0:T(8,128)S(1)} fusion(f32[384,1536]{0,1:T(8,128)} %copy.9, s32[1024]{0:T(1024)S(1)} %pad_clamp_fusion), kind=kCustom, calls=%fused_computation.3 | custom fusion | bytes 787456 | tf_op jit(solution)/shard_map/jit(_take)/gather | solution.py:40
  15.3 0.7 constant_dynamic-slice_fusion.1
  16.0 12.3 %all-to-all-done = f32[4,64,1536]{2,1,0:T(8,128)} async-done(((f32[4,64,1536]{2,1,0:T(8,128)}), f32[4,64,1536]{2,1,0:T(8,128)}, u32[]{:S(2)}, u32[]{:S(2)}) %all-to-all-start) | async-done | bytes 1572896 | tf_op jit(solution)/shard_map/all_to_all | solution.py:9
  28.3 3.0 %copy.6 = f32[256,1536]{0,1:T(8,128)} copy(f32[256,1536]{1,0:T(8,128)} %bitcast.5) | data formatting | bytes 3145728 | tf_op jit(solution)/shard_map/reshape | solution.py:9
  31.3 3.4 %collective-permute-start = (f32[256,1536]{0,1:T(8,128)}, f32[256,1536]{0,1:T(8,128)}, u32[]{:S(2)}, u32[]{:S(2)}) collective-permute-start(f32[256,1536]{0,1:T(8,128)} %copy.6), channel_id=1, source_target_pairs={{0,4},{4,0},{8,12},{12,8},{16,20},{20,16},{24,28},{28,24},{32,36},... | collective-permute-start | bytes 4718600 | tf_op jit(solution)/shard_map/ppermute | solution.py:19
  34.7 0.1 broadcast_select_fusion.4
  34.8 2.9 %broadcast_select_fusion.1 = (f32[384,1536]{1,0:T(8,128)}, f32[384,1536]{1,0:T(8,128)}) fusion(pred[]{:T(512)S(6)} %eq.3, f32[1,384,1536]{2,1,0:T(8,128)S(1)} %copy-done), kind=kLoop, calls=%fused_computation.12 | loop fusion | flops 1179648 | bytes 7077889 | tf_op jit(solution)/shard_map/jit(_where)/select_n | solution.py:55
  37.7 2.4 %gather_fusion.2 = f32[256,256]{1,0:T(8,128)S(1)} fusion(f32[256,1536]{0,1:T(8,128)} %copy.6, s32[1024]{0:T(1024)S(1)} %pad_clamp_fusion.2), kind=kCustom, calls=%fused_computation.clone | custom fusion | bytes 525312 | tf_op jit(solution)/shard_map/jit(_take)/gather | solution.py:38
  40.1 0.0 collective-permute-done
  40.1 2.4 %gather_fusion.3 = f32[256,256]{1,0:T(8,128)S(1)} fusion(f32[256,1536]{0,1:T(8,128)} %collective-permute-done, s32[1024]{0:T(1024)S(1)} %pad_clamp_fusion.1), kind=kCustom, calls=%fused_computation.1.clone | custom fusion | bytes 525312 | tf_op jit(solution)/shard_map/jit(_take)/gather | solution.py:42
  42.5 0.1 bitcast_add_fusion.1
  42.6 0.1 copy.8
  42.8 11.7 %cholesky.50 = f32[128,128]{1,0:T(8,128)S(1)} custom-call(f32[128,128]{1,0:T(8,128)S(1)} %cholesky.118), custom_call_target="Cholesky" | custom-call | tf_op jit(solution)/shard_map/jit(cholesky)/cholesky | solution.py:43
  54.5 0.7 compare_reduce_fusion.1
  55.2 9.8 %custom-call.18 = f32[1,128,128]{1,2,0:T(8,128)S(1)} custom-call(f32[1,128,128]{2,1,0:T(8,128)S(1)} %get-tuple-element.35), custom_call_target="InvertDiagBlocksLowerTriangular" | custom-call | tf_op jit(solution)/shard_map/jit(cholesky)/cholesky | solution.py:43
  65.0 0.2 constant_dynamic-update-slice_fusion
  65.2 0.3 convolution_subtract_fusion.2
  65.5 0.0 copy-start.1
  65.5 11.7 %cholesky.105 = f32[128,128]{1,0:T(8,128)S(1)} custom-call(f32[128,128]{1,0:T(8,128)S(1)} %convolution_subtract_fusion.2), custom_call_target="Cholesky" | custom-call | tf_op jit(solution)/shard_map/jit(cholesky)/cholesky | solution.py:43
  77.3 0.7 compare_reduce_fusion
  79.3 0.1 triangular_solve.70
  79.4 4.2 %while.1 = (s32[]{:T(128)}, f32[256,256]{1,0:T(8,128)S(1)}, s32[2,2]{1,0:T(2,128)S(1)}, f32[2,128,128]{2,1,0:T(8,128)S(1)}, s32[]{:T(128)}) while((s32[]{:T(128)}, f32[256,256]{1,0:T(8,128)S(1)}, s32[2,2]{1,0:T(2,128)S(1)}, f32[2,128,128]{2,1,0:T(8,128)S(1)}, s32[]{:T(128)}) %tuple.28), condition=%wide.while_cond, body=%wide.while_body.sunk | while | flops 2 | bytes 131189 | solution.py:46
  79.6 0.6 fusion.29
  80.2 1.4 %bitcast_dynamic-update-slice_fusion.2 = f32[2,128,128]{2,1,0:T(8,128)S(1)} fusion(f32[2,128,128]{2,1,0:T(8,128)S(1)} %get-tuple-element.77, s32[]{:T(128)S(6)} %copy.17, f32[256,256]{1,0:T(8,128)S(1)} %get-tuple-element.80, s32[]{:T(128)} %bitcast.55, s32[]{:T(128)} %bitcast.56), kind=kLoop, calls=%fused_computation.4.clone.1 | loop fusion | bytes 131084 | tf_op jit(solution)/shard_map/jit(_cho_solve)/triangular_solve
  81.6 0.6 fusion.29
  82.2 1.4 %bitcast_dynamic-update-slice_fusion.2 = f32[2,128,128]{2,1,0:T(8,128)S(1)} fusion(f32[2,128,128]{2,1,0:T(8,128)S(1)} %get-tuple-element.77, s32[]{:T(128)S(6)} %copy.17, f32[256,256]{1,0:T(8,128)S(1)} %get-tuple-element.80, s32[]{:T(128)} %bitcast.55, s32[]{:T(128)} %bitcast.56), kind=kLoop, calls=%fused_computation.4.clone.1 | loop fusion | bytes 131084 | tf_op jit(solution)/shard_map/jit(_cho_solve)/triangular_solve
  83.6 19.7 %custom-call.19 = f32[2,128,128]{1,2,0:T(8,128)S(1)} custom-call(f32[2,128,128]{2,1,0:T(8,128)S(1)} %get-tuple-element.13), custom_call_target="InvertDiagBlocksLowerTriangular" | custom-call | tf_op jit(solution)/shard_map/jit(_cho_solve)/triangular_solve | solution.py:46
  103.3 0.4 fusion.8
  103.7 0.3 convolution_subtract_fusion.1
  104.0 0.4 fusion.15
  104.4 0.3 fusion.14
  104.7 0.4 convolution_subtract_fusion
  105.1 0.3 fusion.13
  105.4 0.0 copy-done.1
  105.4 0.0 copy-start.2
  105.4 0.0 copy-start.3
  105.4 1.8 %broadcast_select_fusion.3 = (f32[256,1536]{0,1:T(8,128)S(1)}, f32[256,1536]{0,1:T(8,128)S(1)}) fusion(f32[256,1536]{0,1:T(8,128)S(1)} %copy-done.1, f32[256,1536]{0,1:T(8,128)} %collective-permute-done, pred[]{:T(512)S(6)} %eq.3), kind=kLoop, calls=%fused_computation.17 | loop fusion | flops 786432 | bytes 6291457 | tf_op jit(solution)/shard_map/jit(_where)/select_n | solution.py:44
  107.2 0.3 copy-done.2
  107.5 0.7 copy-done.3
  108.3 9.9 %fusion = f32[1,384,3072]{2,1,0:T(8,128)} fusion(f32[384,1536]{1,0:T(8,128)S(1)} %copy-done.3, f32[384,1536]{1,0:T(8,128)S(1)} %copy-done.2, f32[256,1536]{0,1:T(8,128)S(1)} %get-tuple-element.29, f32[256,1536]{0,1:T(8,128)S(1)} %get-tuple-element.28, f32[128,384]{1,0:T(8,128)S(1)} %fusion.14, f32[128,384]{1,0:T(8,128)S(1)} %fusion.13), kind=kOutput, calls=%fused_computation.7 | convolution fusion | flops 3627122688 | bytes 12976128 | tf_op jit(solution)/shard_map/dot_general | solution.py:47
  (18 shorter events, 0.2 us)
Async XLA Ops:
  3.5 6.4 %copy-start = (f32[1,384,1536]{2,1,0:T(8,128)S(1)}, f32[1,384,1536]{2,1,0:T(8,128)}, u32[]{:S(2)}) copy-start(f32[1,384,1536]{2,1,0:T(8,128)} %param.4) | copy-start | bytes 7077892
  4.8 23.5 %all-to-all-start = ((f32[4,64,1536]{2,1,0:T(8,128)}), f32[4,64,1536]{2,1,0:T(8,128)}, u32[]{:S(2)}, u32[]{:S(2)}) async-start(f32[4,64,1536]{2,1,0:T(8,128)} %stack.2), calls=%async_computation | async-start | bytes 3145728 | tf_op jit(solution)/shard_map/all_to_all | solution.py:9
  31.3 8.8 %collective-permute-start = (f32[256,1536]{0,1:T(8,128)}, f32[256,1536]{0,1:T(8,128)}, u32[]{:S(2)}, u32[]{:S(2)}) collective-permute-start(f32[256,1536]{0,1:T(8,128)} %copy.6), channel_id=1, source_target_pairs={{0,4},{4,0},{8,12},{12,8},{16,20},{20,16},{24,28},{28,24},{32,36},... | collective-permute-start | bytes 4718600 | tf_op jit(solution)/shard_map/ppermute | solution.py:19
  65.5 39.9 %copy-start.1 = (f32[256,1536]{0,1:T(8,128)S(1)}, f32[256,1536]{0,1:T(8,128)}, u32[]{:S(2)}) copy-start(f32[256,1536]{0,1:T(8,128)} %copy.6) | copy-start | bytes 4718596
  105.4 2.1 %copy-start.2 = (f32[384,1536]{1,0:T(8,128)S(1)}, f32[384,1536]{1,0:T(8,128)}, u32[]{:S(2)}) copy-start(f32[384,1536]{1,0:T(8,128)} %get-tuple-element.30) | copy-start | bytes 7077892
  105.4 2.8 %copy-start.3 = (f32[384,1536]{1,0:T(8,128)S(1)}, f32[384,1536]{1,0:T(8,128)}, u32[]{:S(2)}) copy-start(f32[384,1536]{1,0:T(8,128)} %get-tuple-element.31) | copy-start | bytes 7077892
